TPU v7x, 32 devices: a whole 2x2x4 slice. The times are simulated.
32 devices in a mesh: row: 4 (over x, core), col: 8 (over z, y).
Axes of the slice: x: 2, y: 2, z: 4, core: 2. Of those that a mesh axis runs over, the one named last changes fastest.
Arguments:
- velocity: float32 [3, 2, 128, 512, 256], P(None, None, 'row', 'col'), may hold values from -6 to 6
- register: float32 [3, 2, 128, 512, 256], P(None, None, 'row', 'col'), may hold values from -6 to 6
- offsets: int32 [256], replicated, may hold values from -2 to 2, as said below
- remesh_flag: int32 [256], replicated, may hold values from 0 to 1, as said below
- keep_blocks: int32 [8], replicated, may hold values 0 or 1
Outputs:
- velocity_next: float32 [3, 2, 128, 512, 256], P(None, None, 'row', 'col')
Inputs may be any that keep to these rules, and one draw needn't show every extreme that they name: offsets[j] is 0 or has the sign of ky = j - 128. On each side of ky = 0 the planes of magnitude 1 form one run of consecutive ky, and the planes of magnitude 2 the run that follows it directly, farther from ky = 0. Each of -2, -1, 1 and 2 is carried by half of 32 to 32 planes. Each nonzero value of offsets[j] remesh_flag[j] is taken by at most 32 planes, and in every draw one of them by exactly 32 planes.
All inputs are finite; a program needn't handle non-finite values.
Results may differ from a plain program's by a relative error of at most 0.0055.
Values may be sent and summed in bfloat16 or wider, within the bound.
A program may use at most 192 MiB of HBM per device.

v0:
```python
import math

import jax
import jax.numpy as jnp
from jax import lax
from jax.sharding import PartitionSpec as P

NX = 512
NY = 256
NZ = 256
NZH = 128
MX = 768
MY = 384
MZ = 384


SHEAR_RATE = 40.0
SHEAR_TIME = 0.3
VISCOSITY = 0.0015
TIME_STEP = 0.008
REGISTER_WEIGHT = -153.0 / 128.0
UPDATE_WEIGHT = 8.0 / 15.0
PRODUCT_PAIRS = ((0, 0), (0, 1), (0, 2), (1, 1), (1, 2), (2, 2))
PAIR_LOOKUP = ((0, 1, 2), (1, 3, 4), (2, 4, 5))
OFFSET_VALUES = (-2, -1, 1, 2)


def from_behind(block, axis, distance):
    devices = range(lax.axis_size(axis))
    route = [(i - distance, i) for i in devices if i - distance in devices]
    return lax.ppermute(block, axis, route)


def phase_angles(contracted, produced, period):
    phase_turns = jnp.mod(contracted[:, None] * produced[None, :], period)
    return phase_turns.astype(jnp.float32) * (2.0 * math.pi / period)


def complex_table(contracted, produced, period, direction):
    angles = phase_angles(contracted, produced, period)
    cosine = jnp.cos(angles)
    sine_part = direction * jnp.sin(angles)
    upper_rows = jnp.stack([cosine, sine_part], axis=1)
    lower_rows = jnp.stack([-sine_part, cosine], axis=1)
    return jnp.stack([upper_rows, lower_rows], axis=0).astype(jnp.bfloat16)


def inverse_real_table(mode_list, points, period):
    angles = phase_angles(mode_list, points, period)
    weights = jnp.where(mode_list == 0, 1.0, 2.0).astype(jnp.float32)[:, None]
    return jnp.stack([weights * jnp.cos(angles), -weights * jnp.sin(angles)], axis=0).astype(
        jnp.bfloat16
    )


def forward_real_table(points, mode_list, period):
    angles = phase_angles(points, mode_list, period)
    return jnp.stack([jnp.cos(angles), -jnp.sin(angles)], axis=1).astype(jnp.bfloat16)


def tendency_update(spectra, velocity, register, kx_values, ky_values, kz_values):
    wave_x = kx_values[None, :, None] - SHEAR_TIME * ky_values[None, None, :]
    wave_y = ky_values[None, None, :]
    wave_z = kz_values[:, None, None]
    wave_list = (wave_x, wave_y, wave_z)
    squared = wave_x * wave_x + wave_y * wave_y + wave_z * wave_z
    inverse = 1.0 / jnp.maximum(squared, 1.0)
    advect_real = [
        sum((wave_list[source] * spectra[PAIR_LOOKUP[target][source], 1] for source in range(3)))
        for target in range(3)
    ]
    advect_imag = [
        -sum((wave_list[source] * spectra[PAIR_LOOKUP[target][source], 0] for source in range(3)))
        for target in range(3)
    ]
    diverge_real = sum((wave_list[target] * advect_real[target] for target in range(3)))
    diverge_imag = sum((wave_list[target] * advect_imag[target] for target in range(3)))
    pressure_lift = 2.0 * SHEAR_RATE * wave_y * inverse
    results = []
    for target in range(3):
        halves = []
        for half_index, advect, diverge in (
            (0, advect_real, diverge_real),
            (1, advect_imag, diverge_imag),
        ):
            rate_value = advect[target] - wave_list[target] * diverge * inverse
            rate_value = rate_value + wave_list[target] * pressure_lift * velocity[0, half_index]
            rate_value = rate_value - VISCOSITY * squared * velocity[target, half_index]
            if target == 1:
                rate_value = rate_value - SHEAR_RATE * velocity[0, half_index]
            increment = REGISTER_WEIGHT * register[target, half_index] + TIME_STEP * rate_value
            halves.append(velocity[target, half_index] + UPDATE_WEIGHT * increment)
        results.append(jnp.stack(halves))
    return jnp.stack(results)


def local(velocity, register, offsets, remesh_flag, keep_blocks):
    rows_count = lax.axis_size("row")
    cols_count = lax.axis_size("col")
    row_index = lax.axis_index("row")
    col_index = lax.axis_index("col")
    slab_kz = velocity.shape[2]
    slab_kx = velocity.shape[3]
    y_cols = MY // cols_count
    y_both = y_cols // rows_count
    inverse_scale = 1.0 / math.sqrt(NX * NY * NZ)
    forward_scale = math.sqrt(NX * NY * NZ) / (MX * MY * MZ)
    y_order = jnp.arange(MY, dtype=jnp.int32)
    owner_col = y_order // y_cols
    within_col = y_order % y_cols
    y_permuted = (within_col // y_both * cols_count + owner_col) * y_both + within_col % y_both
    x_points = jnp.arange(MX, dtype=jnp.int32)
    z_points = jnp.arange(MZ, dtype=jnp.int32)
    kx_all = jnp.arange(NX, dtype=jnp.int32) - NX // 2
    ky_all = jnp.arange(NY, dtype=jnp.int32) - NY // 2
    kz_all = jnp.arange(NZH, dtype=jnp.int32)
    kx_local = col_index * slab_kx + jnp.arange(slab_kx, dtype=jnp.int32) - NX // 2
    kz_local = row_index * slab_kz + jnp.arange(slab_kz, dtype=jnp.int32)
    y_inverse = complex_table(ky_all, y_permuted, MY, 1.0)
    x_inverse = complex_table(kx_all, x_points, MX, 1.0)
    z_inverse = inverse_real_table(kz_all, z_points, MZ)
    z_forward = forward_real_table(z_points, kz_all, MZ)
    x_forward = complex_table(x_points, kx_all, MX, -1.0)
    spectral = velocity.astype(jnp.bfloat16)
    along_y = jnp.einsum(
        "crlij,rjsq->csliq", spectral, y_inverse, preferred_element_type=jnp.float32
    ).astype(jnp.bfloat16)
    along_x = jnp.einsum(
        "crliq,risp->cslqp",
        lax.all_to_all(along_y, "col", split_axis=4, concat_axis=3, tiled=True),
        x_inverse,
        preferred_element_type=jnp.float32,
    ).astype(jnp.bfloat16)
    fields = (
        jnp.einsum(
            "crlab,rlz->cabz",
            lax.all_to_all(along_x, "row", split_axis=3, concat_axis=2, tiled=True),
            z_inverse,
            preferred_element_type=jnp.float32,
        )
        * inverse_scale
    )
    products = jnp.stack(
        [fields[left_factor] * fields[right_factor] for left_factor, right_factor in PRODUCT_PAIRS]
    ).astype(jnp.bfloat16)
    modes_z = (
        jnp.einsum("eabz,zsl->esabl", products, z_forward, preferred_element_type=jnp.float32)
        .astype(jnp.bfloat16)
        .reshape(6, 2, y_both, MX, rows_count, slab_kz)
    )
    x_split = x_forward.reshape(2, MX, 2, cols_count, slab_kx)
    arranged = jnp.einsum(
        "eryxab,rxscd->esyacbd", modes_z, x_split, preferred_element_type=jnp.float32
    ).astype(jnp.bfloat16)
    arranged = arranged.reshape(6, 2, y_both, rows_count * cols_count, slab_kz * slab_kx)
    gathered = lax.all_to_all(arranged, ("row", "col"), split_axis=3, concat_axis=2, tiled=True)
    gathered = gathered.reshape(6, 2, MY, slab_kz, slab_kx)
    y_forward = complex_table(y_order, ky_all, MY, -1.0)
    spectra = jnp.einsum(
        "erqli,rqsj->eslij", gathered, y_forward, preferred_element_type=jnp.float32
    )
    spectra = spectra * forward_scale
    updated = tendency_update(
        spectra,
        velocity,
        register,
        kx_local.astype(jnp.float32),
        ky_all.astype(jnp.float32),
        kz_local.astype(jnp.float32),
    )
    moved_by = offsets * remesh_flag
    remeshed = updated * (moved_by == 0).astype(jnp.float32)
    for shift_by in OFFSET_VALUES:
        selected = updated * (moved_by == shift_by).astype(jnp.float32)
        remeshed = remeshed + from_behind(selected, "col", shift_by)
    keep_here = jnp.sum(
        jnp.where(jnp.arange(cols_count, dtype=jnp.int32) == col_index, keep_blocks, 0)
    ).astype(jnp.float32)
    return remeshed * keep_here


def solution(mesh):
    placed = (P(None, None, "row", "col", None), P(None, None, "row", "col", None), P(), P(), P())
    return jax.shard_map(
        local,
        mesh=mesh,
        in_specs=placed,
        out_specs=P(None, None, "row", "col", None),
        check_vma=False,
    )
```

profile of v0, /device:TPU:12, one launch (start us, length us, event | category | flops | bytes accessed | tf_op | source)
XLA Modules:
  0.0 2006.1 jit_solution(4460918960965122890)
XLA Ops:
  2.0 13.6 fusion.10
  15.6 26.8 %copy.79 = bf16[3,2,32,64,384]{3,2,0,1,4:T(8,128)(2,1)} copy(bf16[3,2,32,64,384]{4,3,2,0,1:T(8,128)(2,1)} %fusion.10) | data formatting | bytes 18874368 | tf_op jit(solution)/shard_map/convert_element_type | solution.py:127
  42.4 18.3 reshape.1632
  74.7 194.7 %all-to-all-done = bf16[8,2,294912]{2,1,0:T(2,128)(2,1)} async-done(((bf16[8,2,294912]{2,1,0:T(2,128)(2,1)}), bf16[8,2,294912]{2,1,0:T(2,128)(2,1)}, u32[]{:S(2)}, u32[]{:S(2)}) %all-to-all-start) | async-done | bytes 9437216 | tf_op jit(solution)/shard_map/all_to_all | solution.py:130
  269.4 18.0 reshape.1633
  287.4 20.9 %copy.81 = bf16[3,2,32,8,64,48]{4,3,5,1,2,0:T(8,128)(2,1)} copy(bf16[3,2,32,8,64,48]{4,2,0,1,5,3:T(8,128)(2,1)} %bitcast.330) | data formatting | bytes 18874368 | tf_op jit(solution)/shard_map/all_to_all | solution.py:130
  308.3 25.3 %reshape.1618 = bf16[3,2,32,512,48,1]{3,4,1,2,0,5:T(8,128)(2,1)} reshape(bf16[3,2,32,8,64,48]{4,3,5,1,2,0:T(8,128)(2,1)} %copy.81) | data formatting | bytes 18874368 | tf_op jit(solution)/shard_map/all_to_all | solution.py:130
  333.6 17.1 fusion.9
  350.7 10.5 copy.82
  377.1 146.0 %all-to-all-done.1 = bf16[3,2,32,48,768]{4,2,0,1,3:T(8,128)(2,1)} async-done(((bf16[3,2,32,48,768]{4,2,0,1,3:T(8,128)(2,1)}), bf16[3,2,32,48,768]{4,2,0,1,3:T(8,128)(2,1)}, u32[]{:S(2)}, u32[]{:S(2)}) %all-to-all-start.1) | async-done | bytes 14155808 | tf_op jit(solution)/shard_map/all_to_all | solution.py:137
  523.1 10.6 copy.84
  533.6 24.1 %bitcast_multiply_fusion = f32[3,12,768,384]{3,2,1,0:T(8,128)} fusion(bf16[3,2,128,12,768]{4,2,3,1,0:T(8,128)(2,1)} %bitcast.328, bf16[1,128,384]{2,1,0:T(8,128)(2,1)S(1)} %get-tuple-element.49, bf16[1,128,384]{2,1,0:T(8,128)(2,1)S(1)} %get-tuple-element.50), kind=kOutput, calls=%fused_computation.1 | convolution fusion | flops 5446533120 | bytes 56819712 | tf_op jit(solution)/shard_map/crlab,rlz->cabz/dot_general | solution.py:135
  567.0 12.8 fusion.14
  579.8 12.8 fusion.15
  592.6 9.3 fusion.16
  601.8 12.8 fusion.17
  614.6 9.3 fusion.18
  623.9 28.9 %fusion.6 = bf16[2,128,6,12,768]{4,1,3,2,0:T(8,128)(2,1)} fusion(bf16[6,12,768,384]{3,2,1,0:T(8,128)(2,1)} %fusion.18, bf16[384,1,128]{0,2,1:T(8,128)(2,1)S(1)} %get-tuple-element.51, bf16[384,1,128]{0,2,1:T(8,128)(2,1)S(1)} %get-tuple-element.52), kind=kOutput, calls=%fused_computation.11 | convolution fusion | flops 10886184960 | bytes 70975488 | tf_op jit(solution)/shard_map/eabz,zsl->esabl/dot_general | solution.py:147
  652.8 64.5 %fusion.2 = bf16[6,2,12,4,8,32,64]{6,5,3,2,0,4,1:T(8,128)(2,1)} fusion(bf16[6,2,12,768,4,32,1,1]{3,5,4,2,0,1,7,6:T(8,128)(2,1)} %bitcast.331, bf16[1,768,1,8,64]{1,4,0,3,2:T(8,128)(2,1)S(1)} %get-tuple-element.31, bf16[1,768,1,8,64]{1,4,0,3,2:T(8,128)(2,1)S(1)} %get-tuple-element.30, bf16[1,768,1,8,64]{1,4,0,3,2:T(8,128)(2,1)S(1)} %get-tuple-element.29), kind=kOutput, calls=%fused_computation.4 | convolution fusion | flops 29013049344 | bytes 49545216 | tf_op jit(solution)/shard_map/eryxab,rxscd->esyacbd/dot_general | solution.py:152
  717.4 25.5 %copy.121 = bf16[6,2,12,4,8,32,64]{6,5,1,2,0,4,3:T(8,128)(2,1)} copy(bf16[6,2,12,4,8,32,64]{6,5,3,2,0,4,1:T(8,128)(2,1)} %fusion.2) | data formatting | bytes 37748736 | tf_op jit(solution)/shard_map/reshape | solution.py:155
  742.9 58.3 %reshape.1631 = bf16[6,2,12,32,2048]{4,1,2,0,3:T(2,128)(2,1)} reshape(bf16[6,2,12,4,8,32,64]{6,5,1,2,0,4,3:T(8,128)(2,1)} %copy.121) | data formatting | bytes 37748736 | tf_op jit(solution)/shard_map/reshape | solution.py:155
  810.6 404.3 %all-to-all-done.2 = bf16[6,2,12,32,2048]{4,1,2,0,3:T(2,128)(2,1)} async-done(((bf16[6,2,12,32,2048]{4,1,2,0,3:T(2,128)(2,1)}), bf16[6,2,12,32,2048]{4,1,2,0,3:T(2,128)(2,1)}, u32[]{:S(2)}, u32[]{:S(2)}) %all-to-all-start.2) | async-done | bytes 18874400 | tf_op jit(solution)/shard_map/all_to_all | solution.py:156
  1214.9 17.2 copy.89
  1232.1 59.4 %reshape.1613 = bf16[6,2,384,32,64]{4,3,1,2,0:T(8,128)(2,1)} reshape(bf16[6,2,32,12,1,2048]{5,1,3,2,0,4:T(2,128)(2,1)} %copy.89) | data formatting | bytes 37748736 | tf_op jit(solution)/shard_map/reshape | solution.py:157
  1291.5 45.5 %copy.90 = bf16[6,2,384,32,64]{2,4,1,3,0:T(8,128)(2,1)} copy(bf16[6,2,384,32,64]{4,3,1,2,0:T(8,128)(2,1)} %reshape.1613) | data formatting | bytes 37748736 | tf_op jit(solution)/shard_map/reshape | solution.py:157
  1337.0 20.3 %fusion.3 = f32[6,2,32,64,256]{4,3,2,0,1:T(8,128)} fusion(bf16[6,2,384,32,64]{2,4,1,3,0:T(8,128)(2,1)} %copy.90, bf16[1,384,2,256]{3,1,0,2:T(8,128)(2,1)S(1)} %get-tuple-element.26, bf16[1,384,2,256]{3,1,0,2:T(8,128)(2,1)S(1)} %get-tuple-element.25), kind=kOutput, calls=%fused_computation.7 | convolution fusion | flops 9671540736 | bytes 44826624 | tf_op jit(solution)/shard_map/erqli,rqsj->eslij/dot_general | solution.py:159
  1357.3 9.9 fusion.41
  1398.7 17.8 broadcast_multiply_fusion.3
  1422.0 13.7 collective-permute-start.1
  1440.8 259.5 %collective-permute-done = f32[3,2,32,64,256]{4,3,2,1,0:T(8,128)} collective-permute-done((f32[3,2,32,64,256]{4,3,2,1,0:T(8,128)}, f32[3,2,32,64,256]{4,3,2,1,0:T(8,128)}, u32[]{:S(2)}, u32[]{:S(2)}) %collective-permute-start) | collective-permute-done | bytes 12582944 | tf_op jit(solution)/shard_map/ppermute | solution.py:31
  1700.3 274.5 %collective-permute-done.1 = f32[3,2,32,64,256]{4,3,2,1,0:T(8,128)} collective-permute-done((f32[3,2,32,64,256]{4,3,2,1,0:T(8,128)}, f32[3,2,32,64,256]{4,3,2,1,0:T(8,128)}, u32[]{:S(2)}, u32[]{:S(2)}) %collective-permute-start.1) | collective-permute-done | bytes 12582944 | tf_op jit(solution)/shard_map/ppermute | solution.py:31
  1978.9 26.7 %add_multiply_fusion = f32[3,2,32,64,256]{4,3,2,1,0:T(8,128)} fusion(f32[3,2,32,64,256]{4,3,2,1,0:T(8,128)} %collective-permute-done.3, f32[3,2,32,64,256]{4,3,2,1,0:T(8,128)} %collective-permute-done.2, f32[3,2,32,64,256]{4,3,2,1,0:T(8,128)} %collective-permute-done.1, f32[3,2,32,64,256]{4,3,2,1,0:T(8,128)} %collective-permute-done, ...), kind=kLoop, calls=%fused_computation.20 | loop fusion | flops 25165824 | bytes 75498496 | tf_op jit(solution)/shard_map/mul | solution.py:179
  (75 shorter events, 95.9 us)
Async XLA Ops:
  0.0 1.9 copy-start.9
  60.7 208.7 %all-to-all-start = ((bf16[8,2,294912]{2,1,0:T(2,128)(2,1)}), bf16[8,2,294912]{2,1,0:T(2,128)(2,1)}, u32[]{:S(2)}, u32[]{:S(2)}) async-start(bf16[8,2,294912]{2,1,0:T(2,128)(2,1)} %reshape.1632), calls=%async_computation | async-start | bytes 18874368 | tf_op jit(solution)/shard_map/all_to_all | solution.py:130
  361.2 161.9 %all-to-all-start.1 = ((bf16[3,2,32,48,768]{4,2,0,1,3:T(8,128)(2,1)}), bf16[3,2,32,48,768]{4,2,0,1,3:T(8,128)(2,1)}, u32[]{:S(2)}, u32[]{:S(2)}) async-start(bf16[3,2,32,48,768]{4,2,0,1,3:T(8,128)(2,1)} %copy.82), calls=%async_computation.1 | async-start | bytes 28311552 | tf_op jit(solution)/shard_map/all_to_all | solution.py:137
  801.2 7.5 copy-start.10
  801.2 9.4 copy-start.11
  801.2 9.4 copy-start.12
  801.2 413.8 %all-to-all-start.2 = ((bf16[6,2,12,32,2048]{4,1,2,0,3:T(2,128)(2,1)}), bf16[6,2,12,32,2048]{4,1,2,0,3:T(2,128)(2,1)}, u32[]{:S(2)}, u32[]{:S(2)}) async-start(bf16[6,2,12,32,2048]{4,1,2,0,3:T(2,128)(2,1)} %reshape.1631), calls=%async_computation.2 | async-start | bytes 37748736 | tf_op jit(solution)/shard_map/all_to_all | solution.py:156
  1357.3 15.3 copy-start.3
  1378.8 2.4 copy-start.7
  1378.8 3.7 copy-start.8
  1378.8 10.4 slice-start
  1379.1 18.1 copy-start
  1382.5 6.7 slice-start.1
  1382.5 7.5 slice-start.2
  1382.5 8.1 copy-start.4
  1382.5 8.7 copy-start.5
  1382.5 9.3 copy-start.6
  1396.6 2.0 copy-start.1
  1397.1 19.4 copy-start.2
  1398.7 40.9 %copy-start.13 = (s32[8]{0:T(128)S(1)}, s32[8]{0:T(128)}, u32[]{:S(2)}) copy-start(s32[8]{0:T(128)} %param.9) | copy-start | bytes 100
  1416.5 283.8 %collective-permute-start = (f32[3,2,32,64,256]{4,3,2,1,0:T(8,128)}, f32[3,2,32,64,256]{4,3,2,1,0:T(8,128)}, u32[]{:S(2)}, u32[]{:S(2)}) collective-permute-start(f32[3,2,32,64,256]{4,3,2,1,0:T(8,128)} %get-tuple-element.19), channel_id=1, source_target_pairs={{2,0},{3,1},{4,2},{5,3},{6,4},{7,5},{10,8},{11,9},{12,10},{13,11},... | collective-permute-start | bytes 37748744 | tf_op jit(solution)/shard_map/ppermute | solution.py:31
  1422.0 552.9 %collective-permute-start.1 = (f32[3,2,32,64,256]{4,3,2,1,0:T(8,128)}, f32[3,2,32,64,256]{4,3,2,1,0:T(8,128)}, u32[]{:S(2)}, u32[]{:S(2)}) collective-permute-start(f32[3,2,32,64,256]{4,3,2,1,0:T(8,128)} %get-tuple-element.20), channel_id=1, source_target_pairs={{1,0},{2,1},{3,2},{4,3},{5,4},{6,5},{7,6},{9,8},{10,9},{11,10},{12... | collective-permute-start | bytes 37748744 | tf_op jit(solution)/shard_map/ppermute | solution.py:31
  1435.7 543.3 %collective-permute-start.2 = (f32[3,2,32,64,256]{4,3,2,1,0:T(8,128)}, f32[3,2,32,64,256]{4,3,2,1,0:T(8,128)}, u32[]{:S(2)}, u32[]{:S(2)}) collective-permute-start(f32[3,2,32,64,256]{4,3,2,1,0:T(8,128)} %get-tuple-element.21), channel_id=1, source_target_pairs={{0,1},{1,2},{2,3},{3,4},{4,5},{5,6},{6,7},{8,9},{9,10},{10,11},{11... | collective-permute-start | bytes 37748744 | tf_op jit(solution)/shard_map/ppermute | solution.py:31
  1437.6 541.3 %collective-permute-start.3 = (f32[3,2,32,64,256]{4,3,2,1,0:T(8,128)}, f32[3,2,32,64,256]{4,3,2,1,0:T(8,128)}, u32[]{:S(2)}, u32[]{:S(2)}) collective-permute-start(f32[3,2,32,64,256]{4,3,2,1,0:T(8,128)} %get-tuple-element.22), channel_id=1, source_target_pairs={{0,2},{1,3},{2,4},{3,5},{4,6},{5,7},{8,10},{9,11},{10,12},{11,13},... | collective-permute-start | bytes 37748744 | tf_op jit(solution)/shard_map/ppermute | solution.py:31
where the time goes:
time: 2020 us; the launch traced here: 2010 us
  waiting for transfers between devices  1280 us (63%)
  local copies, waits for them, and re-layouts  349 us (17%)
  matrix products  169 us (8%)
  other arithmetic  160 us (8%)
  starting transfers between devices  43.9 us (2%)
    ppermute x4, waiting for transfers between devices, from_behind(): return lax.ppermute(block, axis, route)  538 us
    all_to_all x1, waiting for transfers between devices, local(): lax.all_to_all(arranged, ('row', 'col'), split_axis=3, concat_axis=2, til...  404 us
    all_to_all x1, waiting for transfers between devices, local(): lax.all_to_all(along_y, 'col', split_axis=4, concat_axis=3, tiled=True)  195 us
    all_to_all x1, waiting for transfers between devices, local(): lax.all_to_all(along_x, 'row', split_axis=3, concat_axis=2, tiled=True)  146 us
    reshape x2, local copies, waits for them, and re-layouts, local(): gathered = gathered.reshape(6, 2, MY, slab_kz, slab_kx)  105 us
    reshape x2, local copies, waits for them, and re-layouts, local(): arranged.reshape(6, 2, y_both, rows_count * cols_count, slab_kz * slab_kx)  83.8 us
    dot_general x1, matrix products, local(): jnp.einsum('eryxab,rxscd->esyacbd', modes_z, x_split, preferred_element_t...  64.5 us
    unnamed x6, other arithmetic  56.9 us
  transfers between devices with their start and end apart: 7, of which 6 were waited for; matrix products, arithmetic and copies ran while one was open for 1% of the time, Pallas kernels for 0%

commit v1 on v0

v1 whole, which is shorter than its diff:
```python
import functools
import math

import jax
import jax.numpy as jnp
from jax import lax
from jax.experimental import pallas as pl
from jax.experimental.pallas import tpu as pltpu
from jax.sharding import PartitionSpec as P

SHEAR_RATE = 40.0
SHEAR_TIME = 0.3
VISCOSITY = 0.0015
TIME_STEP = 0.008
REGISTER_WEIGHT = -153.0 / 128.0
UPDATE_WEIGHT = 8.0 / 15.0
OFFSET_VALUES = (-2, -1, 1, 2)
SHIFT_CAP = 32
SENT_PRODUCTS = 5
CHUNKS = 2
VMEM_LIMIT = 60 * 1024 * 1024


def from_behind(block, axis, distance):
    devices = range(lax.axis_size(axis))
    route = [(i - distance, i) for i in devices if i - distance in devices]
    return lax.ppermute(block, axis, route)


def cosine_turns(turns, period):
    turns = jnp.mod(turns, period)
    return jnp.cos(turns.astype(jnp.float32) * (2.0 * math.pi / period))


def split_rows(count, parts):
    base = count // parts
    sizes = [base + (1 if k >= parts - count % parts else 0) for k in range(parts)]
    return [s for s in sizes if s > 0]


def call(body, grid, in_specs, out_specs, out_shape, scratch=(), flops=0, moved=0, name=None):
    return pl.pallas_call(
        body,
        grid=grid,
        in_specs=in_specs,
        out_specs=out_specs,
        out_shape=out_shape,
        scratch_shapes=list(scratch),
        compiler_params=pltpu.CompilerParams(vmem_limit_bytes=VMEM_LIMIT),
        cost_estimate=pl.CostEstimate(flops=flops, bytes_accessed=moved, transcendentals=0),
        name=name,
    )


def y_inverse_body(table_ref, velocity_ref, out_ref, hold):
    slabs = velocity_ref.shape[2]
    for l in range(slabs):
        real = velocity_ref[0, 0, l].astype(jnp.bfloat16)
        imag = velocity_ref[0, 1, l].astype(jnp.bfloat16)
        straight = jnp.concatenate([real, imag], axis=0)
        turned = jnp.concatenate([-imag, real], axis=0)
        both = jnp.concatenate([straight, turned], axis=1)
        hold[l] = lax.dot_general(
            table_ref[...], both, (((1,), (1,)), ((), ())), preferred_element_type=jnp.float32
        )
    for d in range(out_ref.shape[0]):
        count = out_ref.shape[2]
        piece = hold[:, d * count : (d + 1) * count, :]
        out_ref[d, 0] = jnp.swapaxes(piece, 0, 1).astype(jnp.bfloat16)


def y_inverse(velocity, table, devices, slab_y):
    comps, _, kz, kx, ky = velocity.shape
    block = min(16, kz)
    return call(
        y_inverse_body,
        (comps, kz // block),
        [
            pl.BlockSpec(table.shape, lambda c, l: (0, 0)),
            pl.BlockSpec((1, 2, block, kx, ky), lambda c, l: (c, 0, l, 0, 0)),
        ],
        pl.BlockSpec((devices, 1, slab_y, block, 2 * kx), lambda c, l: (0, c, 0, l, 0)),
        jax.ShapeDtypeStruct((devices, comps, slab_y, kz, 2 * kx), jnp.bfloat16),
        [pltpu.VMEM((block, devices * slab_y, 2 * kx), jnp.float32)],
        flops=8 * comps * kz * kx * ky * devices * slab_y,
        moved=velocity.size * 4 + devices * comps * slab_y * kz * kx * 4,
        name="y_inverse",
    )(table, velocity)


def grid_body(scale, in_ref, xi_ref, zi_ref, zf_ref, xf_ref, out_ref, rows_in, fields, rows_out):
    rows, cols, comps, _, kz, width = in_ref.shape
    modes = rows * kz
    for c in range(comps):
        for r in range(rows):
            for q in range(cols):
                rows_in[c * modes + r * kz : c * modes + (r + 1) * kz, q * width : (q + 1) * width] = (
                    in_ref[r, q, c, 0]
                )
    points = xi_ref.shape[1] // 2
    for c in range(comps):
        along = jnp.dot(
            rows_in[c * modes : (c + 1) * modes, :], xi_ref[...], preferred_element_type=jnp.float32
        ).astype(jnp.bfloat16)
        stacked = jnp.concatenate([along[:, :points], along[:, points:]], axis=0)
        fields[c] = jnp.dot(zi_ref[...], stacked, preferred_element_type=jnp.float32) * scale
    for e in range(out_ref.shape[2]):
        if e == 0:
            product = fields[0] * fields[0] - fields[2] * fields[2]
        elif e == 1:
            product = fields[0] * fields[1]
        elif e == 2:
            product = fields[0] * fields[2]
        elif e == 3:
            product = fields[1] * fields[1] - fields[2] * fields[2]
        else:
            product = fields[1] * fields[2]
        modes_z = jnp.dot(
            zf_ref[...], product.astype(jnp.bfloat16), preferred_element_type=jnp.float32
        ).astype(jnp.bfloat16)
        rows_out[:, :points] = modes_z[:modes]
        rows_out[:, points:] = modes_z[modes:]
        result = jnp.dot(rows_out[...], xf_ref[...], preferred_element_type=jnp.float32).astype(
            jnp.bfloat16
        )
        for r in range(rows):
            for q in range(cols):
                out_ref[r, q, e, 0] = result[r * kz : (r + 1) * kz, q * width : (q + 1) * width]


def grid_stage(arrived, xi, zi, zf, xf, scale):
    rows, cols, comps, slab_y, kz, width = arrived.shape
    modes, points, deep = rows * kz, xi.shape[1] // 2, zi.shape[0]
    whole = lambda table: pl.BlockSpec(
        table.shape, lambda y: (0, 0), pipeline_mode=pl.Buffered(1)
    )
    work = comps * modes * xi.size + comps * zi.size * points
    work += SENT_PRODUCTS * (zf.size * points + modes * xf.size)
    return call(
        functools.partial(grid_body, scale),
        (slab_y,),
        [
            pl.BlockSpec((rows, cols, comps, 1, kz, width), lambda y: (0, 0, 0, y, 0, 0)),
            whole(xi),
            whole(zi),
            whole(zf),
            whole(xf),
        ],
        pl.BlockSpec((rows, cols, SENT_PRODUCTS, 1, kz, width), lambda y: (0, 0, 0, y, 0, 0)),
        jax.ShapeDtypeStruct((rows, cols, SENT_PRODUCTS, slab_y, kz, width), jnp.bfloat16),
        [
            pltpu.VMEM((comps * modes, cols * width), jnp.bfloat16),
            pltpu.VMEM((comps, deep, points), jnp.float32),
            pltpu.VMEM((modes, 2 * points), jnp.bfloat16),
        ],
        flops=2 * slab_y * work,
        moved=arrived.size * 6,
        name="grid_stage",
    )(arrived, xi, zi, zf, xf)


def update_body(parts, scale, kz_block, *refs):
    gathered = refs[:parts]
    tables = refs[parts : 2 * parts]
    velocity_ref, register_ref, pick_ref, updated_ref, picked_ref, hold, spectra = refs[2 * parts :]
    _, _, slabs, kx, ky = velocity_ref.shape
    width = 2 * kx
    for e in range(SENT_PRODUCTS):
        for part in range(parts):
            source = gathered[part]
            devices, _, slab_y, _, _ = source.shape
            for d in range(devices):
                base = d * slab_y
                hold[part][:, base : base + slab_y, :] = jnp.swapaxes(
                    source[d, e].astype(jnp.float32), 0, 1
                )
        for l in range(slabs):
            total = None
            for part in range(parts):
                term = lax.dot_general(
                    hold[part][l].astype(jnp.bfloat16),
                    tables[part][...],
                    (((0,), (0,)), ((), ())),
                    preferred_element_type=jnp.float32,
                )
                total = term if total is None else total + term
            cos_part, sin_part = total[:, :ky], total[:, ky:]
            spectra[e, 0, l] = (cos_part[:kx] + sin_part[kx:]) * scale
            spectra[e, 1, l] = (cos_part[kx:] - sin_part[:kx]) * scale
    kx_first = (lax.axis_index("col") * kx - kx * lax.axis_size("col") // 2).astype(jnp.float32)
    kz_first = (lax.axis_index("row") * kz_block + pl.program_id(0) * slabs).astype(jnp.float32)
    k_y = lax.broadcasted_iota(jnp.int32, (kx, ky), 1).astype(jnp.float32) - float(ky // 2)
    k_x = lax.broadcasted_iota(jnp.int32, (kx, ky), 0).astype(jnp.float32) + kx_first
    k_x = k_x - SHEAR_TIME * k_y
    plane = k_x * k_x + k_y * k_y
    for l in range(slabs):
        k_z = kz_first + float(l)
        squared = plane + k_z * k_z
        inverse = 1.0 / jnp.maximum(squared, 1.0)
        waves = (k_x, k_y, k_z)
        lift = 2.0 * SHEAR_RATE * k_y * inverse
        for half in range(2):
            p = [spectra[e, 1 - half, l] for e in range(SENT_PRODUCTS)]
            advect = [
                k_x * p[0] + k_y * p[1] + k_z * p[2],
                k_x * p[1] + k_y * p[3] + k_z * p[4],
                k_x * p[2] + k_y * p[4],
            ]
            if half == 1:
                advect = [-value for value in advect]
            diverge = k_x * advect[0] + k_y * advect[1] + k_z * advect[2]
            first = velocity_ref[0, half, l]
            shared = lift * first - diverge * inverse
            for m in range(3):
                own = first if m == 0 else velocity_ref[m, half, l]
                rate = advect[m] + waves[m] * shared - VISCOSITY * squared * own
                if m == 1:
                    rate = rate - SHEAR_RATE * first
                increment = REGISTER_WEIGHT * register_ref[m, half, l] + TIME_STEP * rate
                updated_ref[m, half, l] = own + UPDATE_WEIGHT * increment
    for m in range(3):
        for half in range(2):
            rounded = updated_ref[m, half].astype(jnp.bfloat16).reshape(slabs * kx, ky)
            chosen = lax.dot_general(
                pick_ref[...], rounded, (((1,), (1,)), ((), ())), preferred_element_type=jnp.float32
            ).astype(jnp.bfloat16)
            for v in range(len(OFFSET_VALUES)):
                picked_ref[v, m, half] = chosen[v * SHIFT_CAP : (v + 1) * SHIFT_CAP]


def update_stage(gathered, tables, velocity, register, pick, scale):
    comps, _, kz, kx, ky = velocity.shape
    block = min(8, kz)
    parts = len(gathered)
    state = pl.BlockSpec((comps, 2, block, kx, ky), lambda l: (0, 0, l, 0, 0))
    shifts = len(OFFSET_VALUES)

    def body(*refs):
        inner = list(refs[: 2 * parts + 5])
        holds = refs[2 * parts + 5 : 3 * parts + 5]
        update_body(parts, scale, kz, *inner, holds, refs[-1])

    in_specs = [
        pl.BlockSpec(g.shape[:3] + (block, g.shape[4]), lambda l: (0, 0, 0, l, 0)) for g in gathered
    ]
    in_specs += [pl.BlockSpec(t.shape, lambda l: (0, 0), pipeline_mode=pl.Buffered(1)) for t in tables]
    in_specs += [state, state, pl.BlockSpec(pick.shape, lambda l: (0, 0))]
    return call(
        body,
        (kz // block,),
        in_specs,
        [
            state,
            pl.BlockSpec((shifts, comps, 2, SHIFT_CAP, block * kx), lambda l: (0, 0, 0, 0, l)),
        ],
        [
            jax.ShapeDtypeStruct(velocity.shape, jnp.float32),
            jax.ShapeDtypeStruct((shifts, comps, 2, SHIFT_CAP, kz * kx), jnp.bfloat16),
        ],
        [pltpu.VMEM((block, t.shape[0], 2 * kx), jnp.float32) for t in tables]
        + [pltpu.VMEM((SENT_PRODUCTS, 2, block, kx, ky), jnp.float32)],
        flops=1,
        moved=velocity.size * 16,
        name="update_stage",
    )(*gathered, *tables, velocity, register, pick)


def remesh_body(shifts, *refs):
    arrived = refs[:shifts]
    updated_ref, pick_ref, stay_ref, keep_ref, out_ref = refs[shifts:]
    comps, _, slabs, kx, ky = updated_ref.shape
    keep = keep_ref[...]
    stay = stay_ref[...] * keep
    for m in range(comps):
        for half in range(2):
            planes = jnp.concatenate([ref[m, half] for ref in arrived], axis=0)
            moved = lax.dot_general(
                planes, pick_ref[...], (((0,), (0,)), ((), ())), preferred_element_type=jnp.float32
            )
            own = updated_ref[m, half].reshape(slabs * kx, ky)
            out_ref[m, half] = (own * stay + moved * keep).reshape(slabs, kx, ky)


def remesh_stage(arrived, updated, pick, stay, keep):
    comps, _, kz, kx, ky = updated.shape
    block = min(8, kz)
    state = pl.BlockSpec((comps, 2, block, kx, ky), lambda l: (0, 0, l, 0, 0))
    planes = pl.BlockSpec((comps, 2, SHIFT_CAP, block * kx), lambda l: (0, 0, 0, l))
    row = pl.BlockSpec((1, ky), lambda l: (0, 0))
    return call(
        functools.partial(remesh_body, len(arrived)),
        (kz // block,),
        [planes] * len(arrived) + [state, pl.BlockSpec(pick.shape, lambda l: (0, 0)), row, row],
        state,
        jax.ShapeDtypeStruct(updated.shape, jnp.float32),
        flops=1,
        moved=updated.size * 10,
        name="remesh_stage",
    )(*arrived, updated, pick, stay, keep)


def local(velocity, register, offsets, remesh_flag, keep_blocks):
    rows = lax.axis_size("row")
    cols = lax.axis_size("col")
    col_index = lax.axis_index("col")
    devices = rows * cols
    comps, _, kz, kx, ny = velocity.shape
    nx, nzh = kx * cols, kz * rows
    nz = 2 * nzh
    mx, my, mz = nx * 3 // 2, ny * 3 // 2, nz * 3 // 2
    slab_y = my // devices
    inverse_scale = 1.0 / math.sqrt(nx * ny * nz)
    forward_scale = math.sqrt(nx * ny * nz) / (mx * my * mz)
    ky_all = jnp.arange(ny, dtype=jnp.int32) - ny // 2
    kz_all = jnp.arange(nzh, dtype=jnp.int32)

    sizes = split_rows(slab_y, CHUNKS)
    y_lists, start = [], 0
    for size in sizes:
        own = jnp.arange(devices, dtype=jnp.int32)[:, None] * slab_y + start
        y_lists.append((own + jnp.arange(size, dtype=jnp.int32)).reshape(-1))
        start += size
    inverse_tables, forward_tables = [], []
    for y_points in y_lists:
        turns = y_points[:, None] * ky_all[None, :]
        cosine = cosine_turns(turns, my)
        sine = cosine_turns(turns - my // 4, my)
        table = jnp.concatenate([cosine, sine], axis=1).astype(jnp.bfloat16)
        inverse_tables.append(table)
        forward_tables.append(table)

    split_index = jnp.arange(2 * nx, dtype=jnp.int32)
    part_kx = split_index // kx % 2
    wave_kx = split_index // (2 * kx) * kx + split_index % kx - nx // 2
    point_index = jnp.arange(2 * mx, dtype=jnp.int32)
    part_x, point_x = point_index // mx, point_index % mx
    turn_x = wave_kx[:, None] * point_x[None, :]
    quarter = part_kx[:, None] - part_x[None, :]
    xi = cosine_turns(turn_x + quarter * (mx // 4), mx).astype(jnp.bfloat16)
    turn_f = point_x[:, None] * wave_kx[None, :]
    quarter_f = part_kx[None, :] - part_x[:, None]
    xf = cosine_turns(turn_f + quarter_f * (mx // 4), mx).astype(jnp.bfloat16)
    z_points = jnp.arange(mz, dtype=jnp.int32)
    turn_z = z_points[:, None] * kz_all[None, :]
    weight = jnp.where(kz_all == 0, 1.0, 2.0).astype(jnp.float32)[None, :]
    cos_z, minus_sin_z = cosine_turns(turn_z, mz), cosine_turns(turn_z + mz // 4, mz)
    zi = jnp.concatenate([weight * cos_z, weight * minus_sin_z], axis=1).astype(jnp.bfloat16)
    zf = jnp.concatenate([cos_z.T, minus_sin_z.T], axis=0).astype(jnp.bfloat16)

    moved_by = offsets * remesh_flag
    picks = []
    for shift_by in OFFSET_VALUES:
        hit = moved_by == shift_by
        place = jnp.cumsum(hit.astype(jnp.int32)) - 1
        slots = jnp.arange(SHIFT_CAP, dtype=jnp.int32)[:, None]
        picks.append((slots == place[None, :]) & hit[None, :])
    pick = jnp.concatenate(picks, axis=0).astype(jnp.bfloat16)
    stay = (moved_by == 0).astype(jnp.float32)[None, :]
    keep_here = jnp.sum(
        jnp.where(jnp.arange(cols, dtype=jnp.int32) == col_index, keep_blocks, 0)
    ).astype(jnp.float32)
    keep = jnp.broadcast_to(keep_here, (1, ny))

    arrived = []
    for table, size in zip(inverse_tables, sizes):
        sent = y_inverse(velocity, table, devices, size)
        sent = lax.all_to_all(sent, ("row", "col"), split_axis=0, concat_axis=0, tiled=True)
        arrived.append(sent.reshape((rows, cols) + sent.shape[1:]))
    gathered = []
    for block in arrived:
        modes = grid_stage(block, xi, zi, zf, xf, inverse_scale)
        modes = modes.reshape((devices,) + modes.shape[2:])
        gathered.append(
            lax.all_to_all(modes, ("row", "col"), split_axis=0, concat_axis=0, tiled=True)
        )
    updated, picked = update_stage(
        gathered, forward_tables, velocity, register, pick, forward_scale
    )
    received = [from_behind(picked[v], "col", OFFSET_VALUES[v]) for v in range(len(OFFSET_VALUES))]
    return remesh_stage(received, updated, pick, stay, keep)


def solution(mesh):
    placed = (P(None, None, "row", "col", None), P(None, None, "row", "col", None), P(), P(), P())
    return jax.shard_map(
        local,
        mesh=mesh,
        in_specs=placed,
        out_specs=P(None, None, "row", "col", None),
        check_vma=False,
    )
```

time: 2020 us -> 697 us (0.35)
  waiting for transfers between devices: 1280 us -> 428 us
  local copies, waits for them, and re-layouts: 349 us -> 5.81 us
  matrix products: 169 us -> 0 us
  Pallas kernels: 0 us -> 145 us
  other arithmetic: 160 us -> 65.6 us
    ppermute x4, waiting for transfers between devices: 538 us -> 31.9 us  [from_behind(): return lax.ppermute(block, axis, route)]
    all_to_all x3 -> x4, waiting for transfers between devices: 745 us -> 396 us  [the longest x2 298 us: local(): lax.all_to_all(modes, ('row', 'col'), split_axis=0, concat_axis=0, tiled=...]
    reshape x4 -> x0, local copies, waits for them, and re-layouts: 189 us -> none  [the longest x2 105 us: local(): gathered = gathered.reshape(6, 2, MY, slab_kz, slab_kx)]
    dot_general x6 -> x0, matrix products: 169 us -> none  [the longest x1 64.5 us: local(): jnp.einsum('eryxab,rxscd->esyacbd', modes_z, x_split, preferred_element_t...]
    pallas_call x0 -> x6, Pallas kernels: none -> 145 us  [the longest x2 77.7 us: grid_stage(): call(functools.partial(grid_body, scale), (slab_y,), [pl.BlockSpec((rows,...]
    all_to_all x4 -> x0, local copies, waits for them, and re-layouts: 73.9 us -> none  [the longest x2 46.2 us: local(): lax.all_to_all(along_y, 'col', split_axis=4, concat_axis=3, tiled=True)]
    unnamed x6 -> x0, other arithmetic: 56.9 us -> none
    convert_element_type x5 -> x3, other arithmetic: 0.03 us -> 53.5 us  [the longest x1 26.7 us: local(): xf = cosine_turns(turn_f + quarter_f * (mx // 4), mx).astype(jnp.bfloat16)]
  transfers between devices with their start and end apart: 7 -> 8, of which waited for: 6 -> 7; matrix products, arithmetic and copies ran while one was open for 1% -> 9% of each run, Pallas kernels for 0% -> 13%
where the time goes in v1:
time: 697 us; the launch traced here: 696 us
  waiting for transfers between devices  428 us (61%)
  Pallas kernels  145 us (21%)
  other arithmetic  65.6 us (9%)
  starting transfers between devices  50.5 us (7%)
    all_to_all x2, waiting for transfers between devices, local(): lax.all_to_all(modes, ('row', 'col'), split_axis=0, concat_axis=0, tiled=...  298 us
    all_to_all x2, waiting for transfers between devices, local(): lax.all_to_all(sent, ('row', 'col'), split_axis=0, concat_axis=0, tiled=T...  97.9 us
    pallas_call x2, Pallas kernels, grid_stage(): call(functools.partial(grid_body, scale), (slab_y,), [pl.BlockSpec((rows,...  77.7 us
    pallas_call x1, Pallas kernels, update_stage(): call(body, (kz // block,), in_specs, [state, pl.BlockSpec((shifts, comps,...  34.1 us
    ppermute x4, waiting for transfers between devices, from_behind(): return lax.ppermute(block, axis, route)  31.9 us
    convert_element_type x1, other arithmetic, local(): xf = cosine_turns(turn_f + quarter_f * (mx // 4), mx).astype(jnp.bfloat16)  26.7 us
    convert_element_type x1, other arithmetic, local(): xi = cosine_turns(turn_x + quarter * (mx // 4), mx).astype(jnp.bfloat16)  26.2 us
    pallas_call x2, Pallas kernels, y_inverse(): call(y_inverse_body, (comps, kz // block), [pl.BlockSpec(table.shape, lam...  22.4 us
  transfers between devices with their start and end apart: 8, of which 7 were waited for; matrix products, arithmetic and copies ran while one was open for 9% of the time, Pallas kernels for 13%

profile of v1, /device:TPU:12, one launch (start us, length us, event | category | flops | bytes accessed | tf_op | source)
XLA Modules:
  0.0 695.9 jit_solution(9581908029187724705)
XLA Ops:
  0.4 3.2 fusion.53
  3.6 0.7 pad_maximum_fusion.3.table_ref.refs_3_
  4.3 11.3 %y_inverse.3 = bf16[32,3,6,32,128]{4,3,2,1,0:T(8,128)(2,1)} custom-call(bf16[192,512]{1,0:T(8,128)(2,1)} %pad_maximum_fusion.3.table_ref.refs_3_, f32[3,2,32,64,256]{4,3,2,1,0:T(8,128)} %refs_4_.1), custom_call_target="tpu_custom_call" | custom-call | flops 2415919104 | bytes 17301504 | tf_op jit(solution)/shard_map/y_inverse/pallas_call | solution.py:75
  15.6 6.0 all-to-all-start.2
  21.6 0.7 pad_maximum_fusion.table_ref.refs_2_
  22.3 11.2 %y_inverse.2 = bf16[32,3,6,32,128]{4,3,2,1,0:T(8,128)(2,1)} custom-call(bf16[192,512]{1,0:T(8,128)(2,1)} %pad_maximum_fusion.table_ref.refs_2_, f32[3,2,32,64,256]{4,3,2,1,0:T(8,128)} %refs_4_.1), custom_call_target="tpu_custom_call" | custom-call | flops 2415919104 | bytes 17301504 | tf_op jit(solution)/shard_map/y_inverse/pallas_call | solution.py:75
  33.5 91.2 %all-to-all-done.2 = bf16[32,3,6,32,128]{4,3,2,1,0:T(8,128)(2,1)} async-done(((bf16[32,3,6,32,128]{4,3,2,1,0:T(8,128)(2,1)}), bf16[32,3,6,32,128]{4,3,2,1,0:T(8,128)(2,1)}, u32[]{:S(2)}, u32[]{:S(2)}) %all-to-all-start.2) | async-done | bytes 4718624 | tf_op jit(solution)/shard_map/all_to_all | solution.py:367
  124.6 7.7 %all-to-all-start = ((bf16[32,3,6,32,128]{4,3,2,1,0:T(8,128)(2,1)}), bf16[32,3,6,32,128]{4,3,2,1,0:T(8,128)(2,1)}, u32[]{:S(2)}, u32[]{:S(2)}) async-start(bf16[32,3,6,32,128]{4,3,2,1,0:T(8,128)(2,1)} %y_inverse.2), calls=%async_computation | async-start | bytes 9437184 | tf_op jit(solution)/shard_map/all_to_all | solution.py:367
  132.4 1.5 fusion.45
  133.9 1.5 fusion.36
  135.4 0.7 pad_maximum_fusion.1.zi_ref
  136.1 0.7 pad_maximum_fusion.2.zf_ref
  136.9 26.2 %fusion.3.xi_ref = bf16[1024,1536]{1,0:T(8,128)(2,1)} fusion(s32[1536]{0:T(1024)S(1)} %get-tuple-element.37, s32[1024]{0:T(1024)S(1)} %get-tuple-element.39, s32[1536]{0:T(1024)S(1)} %get-tuple-element.38, s32[1024]{0:T(1024)S(1)} %get-tuple-element.40), kind=kLoop, calls=%fused_computation.5 | loop fusion | flops 20447232 | bytes 3166208 | tf_op jit(solution)/shard_map/convert_element_type | solution.py:339
  163.0 26.7 %fusion.7.xf_ref = bf16[1536,1024]{1,0:T(8,128)(2,1)} fusion(s32[1536]{0:T(1024)S(1)} %get-tuple-element.37, s32[1024]{0:T(1024)S(1)} %get-tuple-element.39, s32[1024]{0:T(1024)S(1)} %get-tuple-element.40, s32[1536]{0:T(1024)S(1)} %get-tuple-element.38), kind=kLoop, calls=%fused_computation.9 | loop fusion | flops 20447232 | bytes 3166208 | tf_op jit(solution)/shard_map/convert_element_type | solution.py:342
  189.8 38.9 %grid_stage.3 = bf16[4,8,5,6,32,128]{5,4,3,2,1,0:T(8,128)(2,1)} custom-call(bf16[4,8,3,6,32,128]{5,4,3,2,1,0:T(8,128)(2,1)} %bitcast.2.in_ref, bf16[1024,1536]{1,0:T(8,128)(2,1)} %fusion.3.xi_ref, bf16[384,256]{1,0:T(8,128)(2,1)} %pad_maximum_fusion.1.zi_ref, bf16[256,384]{1,0:T(8,128)(2,1)} %pad_maximum_fusion.2.zf_ref, bf16[1536,1024]{1,0:T(8,128)(2,1)} %fusion.7.xf_ref), custom_call_target="tpu_custom_call" | custom-call | flops 26575110144 | bytes 14155776 | tf_op jit(solution)/shard_map/grid_stage/pallas_call | solution.py:139
  228.6 6.7 all-to-all-done
  235.4 7.9 %all-to-all-start.3 = ((bf16[32,5,6,32,128]{4,3,2,1,0:T(8,128)(2,1)}), bf16[32,5,6,32,128]{4,3,2,1,0:T(8,128)(2,1)}, u32[]{:S(2)}, u32[]{:S(2)}) async-start(bf16[32,5,6,32,128]{4,3,2,1,0:T(8,128)(2,1)} %bitcast.30), calls=%async_computation.3 | async-start | bytes 15728640 | tf_op jit(solution)/shard_map/all_to_all | solution.py:374
  243.3 38.9 %grid_stage.2 = bf16[4,8,5,6,32,128]{5,4,3,2,1,0:T(8,128)(2,1)} custom-call(bf16[4,8,3,6,32,128]{5,4,3,2,1,0:T(8,128)(2,1)} %bitcast.in_ref, bf16[1024,1536]{1,0:T(8,128)(2,1)} %fusion.3.xi_ref, bf16[384,256]{1,0:T(8,128)(2,1)} %pad_maximum_fusion.1.zi_ref, bf16[256,384]{1,0:T(8,128)(2,1)} %pad_maximum_fusion.2.zf_ref, bf16[1536,1024]{1,0:T(8,128)(2,1)} %fusion.7.xf_ref), custom_call_target="tpu_custom_call" | custom-call | flops 26575110144 | bytes 14155776 | tf_op jit(solution)/shard_map/grid_stage/pallas_call | solution.py:139
  282.2 131.6 %all-to-all-done.3.refs_1_ = bf16[32,5,6,32,128]{4,3,2,1,0:T(8,128)(2,1)} async-done(((bf16[32,5,6,32,128]{4,3,2,1,0:T(8,128)(2,1)}), bf16[32,5,6,32,128]{4,3,2,1,0:T(8,128)(2,1)}, u32[]{:S(2)}, u32[]{:S(2)}) %all-to-all-start.3) | async-done | bytes 7864352 | tf_op jit(solution)/shard_map/all_to_all | solution.py:374
  413.8 12.0 %all-to-all-start.1 = ((bf16[32,5,6,32,128]{4,3,2,1,0:T(8,128)(2,1)}), bf16[32,5,6,32,128]{4,3,2,1,0:T(8,128)(2,1)}, u32[]{:S(2)}, u32[]{:S(2)}) async-start(bf16[32,5,6,32,128]{4,3,2,1,0:T(8,128)(2,1)} %bitcast.29), calls=%async_computation.1 | async-start | bytes 15728640 | tf_op jit(solution)/shard_map/all_to_all | solution.py:374
  429.4 166.8 %all-to-all-done.1.refs_0_ = bf16[32,5,6,32,128]{4,3,2,1,0:T(8,128)(2,1)} async-done(((bf16[32,5,6,32,128]{4,3,2,1,0:T(8,128)(2,1)}), bf16[32,5,6,32,128]{4,3,2,1,0:T(8,128)(2,1)}, u32[]{:S(2)}, u32[]{:S(2)}) %all-to-all-start.1) | async-done | bytes 7864352 | tf_op jit(solution)/shard_map/all_to_all | solution.py:374
  596.2 34.1 %update_stage.1 = (f32[3,2,32,64,256]{4,3,2,1,0:T(8,128)}, bf16[4,3,2,32,2048]{4,3,2,1,0:T(8,128)(2,1)}) custom-call(bf16[32,5,6,32,128]{4,3,2,1,0:T(8,128)(2,1)} %all-to-all-done.1.refs_0_, bf16[32,5,6,32,128]{4,3,2,1,0:T(8,128)(2,1)} %all-to-all-done.3.refs_1_, bf16[192,512]{1,0:T(8,128)(2,1)} %pad_maximum_fusion.table_ref.refs_2_, ...), custom_call_target="tpu_custom_call" | custom-call | flops 1 | bytes 50331648 | tf_op jit(solution)/shard_map/update_stage/pallas_call | solution.py:248
  630.3 3.7 slice_bitcast_fusion
  634.0 4.2 collective-permute-start
  638.3 8.7 %collective-permute-start.1 = (bf16[3,2,32,2048]{3,2,1,0:T(8,128)(2,1)}, bf16[3,2,32,2048]{3,2,1,0:T(8,128)(2,1)S(1)}, u32[]{:S(2)}, u32[]{:S(2)}) collective-permute-start(bf16[3,2,32,2048]{3,2,1,0:T(8,128)(2,1)} %get-tuple-element.21), channel_id=1, source_target_pairs={{1,0},{2,1},{3,2},{4,3},{5,4},{6,5},{7,6},{9,8},{10,9},{11,10},{12... | collective-permute-start | bytes 2359304 | tf_op jit(solution)/shard_map/ppermute | solution.py:27
  647.0 1.9 collective-permute-start.2
  648.9 1.9 collective-permute-start.3
  650.8 0.6 fusion.98
  652.1 6.1 collective-permute-done.refs_0_
  658.2 21.8 %collective-permute-done.1.refs_1_ = bf16[3,2,32,2048]{3,2,1,0:T(8,128)(2,1)S(1)} collective-permute-done((bf16[3,2,32,2048]{3,2,1,0:T(8,128)(2,1)}, bf16[3,2,32,2048]{3,2,1,0:T(8,128)(2,1)S(1)}, u32[]{:S(2)}, u32[]{:S(2)}) %collective-permute-start.1) | collective-permute-done | bytes 786464 | tf_op jit(solution)/shard_map/ppermute | solution.py:27
  680.0 4.0 collective-permute-done.2.refs_2_
  685.2 10.8 %remesh_stage.1 = f32[3,2,32,64,256]{4,3,2,1,0:T(8,128)} custom-call(bf16[3,2,32,2048]{3,2,1,0:T(8,128)(2,1)} %copy-done, bf16[3,2,32,2048]{3,2,1,0:T(8,128)(2,1)} %copy-done.1, bf16[3,2,32,2048]{3,2,1,0:T(8,128)(2,1)} %copy-done.2, bf16[3,2,32,2048]{3,2,1,0:T(8,128)(2,1)} %copy-done.3, f32[3,2,32,64,256]{4,3,2,1,0:T(8,128)} %get-tuple-element.8.refs_4_, ...), custom_call_target="tpu_custom_call" | custom-call | flops 1 | bytes 31457280 | tf_op jit(solution)/shard_map/remesh_stage/pallas_call | solution.py:290
  (51 shorter events, 5.2 us)
Async XLA Ops:
  15.6 109.1 %all-to-all-start.2 = ((bf16[32,3,6,32,128]{4,3,2,1,0:T(8,128)(2,1)}), bf16[32,3,6,32,128]{4,3,2,1,0:T(8,128)(2,1)}, u32[]{:S(2)}, u32[]{:S(2)}) async-start(bf16[32,3,6,32,128]{4,3,2,1,0:T(8,128)(2,1)} %y_inverse.3), calls=%async_computation.2 | async-start | bytes 9437184 | tf_op jit(solution)/shard_map/all_to_all | solution.py:367
  124.6 110.7 %all-to-all-start = ((bf16[32,3,6,32,128]{4,3,2,1,0:T(8,128)(2,1)}), bf16[32,3,6,32,128]{4,3,2,1,0:T(8,128)(2,1)}, u32[]{:S(2)}, u32[]{:S(2)}) async-start(bf16[32,3,6,32,128]{4,3,2,1,0:T(8,128)(2,1)} %y_inverse.2), calls=%async_computation | async-start | bytes 9437184 | tf_op jit(solution)/shard_map/all_to_all | solution.py:367
  235.4 178.4 %all-to-all-start.3 = ((bf16[32,5,6,32,128]{4,3,2,1,0:T(8,128)(2,1)}), bf16[32,5,6,32,128]{4,3,2,1,0:T(8,128)(2,1)}, u32[]{:S(2)}, u32[]{:S(2)}) async-start(bf16[32,5,6,32,128]{4,3,2,1,0:T(8,128)(2,1)} %bitcast.30), calls=%async_computation.3 | async-start | bytes 15728640 | tf_op jit(solution)/shard_map/all_to_all | solution.py:374
  413.8 12.0 %copy-start.4 = (s32[256]{0:T(256)S(1)}, s32[256]{0:T(256)}, u32[]{:S(2)}) copy-start(s32[256]{0:T(256)} %param.7) | copy-start | bytes 3076
  413.8 12.0 %copy-start.5 = (s32[256]{0:T(256)S(1)}, s32[256]{0:T(256)}, u32[]{:S(2)}) copy-start(s32[256]{0:T(256)} %param.8) | copy-start | bytes 3076
  413.8 182.4 %all-to-all-start.1 = ((bf16[32,5,6,32,128]{4,3,2,1,0:T(8,128)(2,1)}), bf16[32,5,6,32,128]{4,3,2,1,0:T(8,128)(2,1)}, u32[]{:S(2)}, u32[]{:S(2)}) async-start(bf16[32,5,6,32,128]{4,3,2,1,0:T(8,128)(2,1)} %bitcast.29), calls=%async_computation.1 | async-start | bytes 15728640 | tf_op jit(solution)/shard_map/all_to_all | solution.py:374
  630.3 20.5 %copy-start.6 = (s32[8]{0:T(128)S(1)}, s32[8]{0:T(128)}, u32[]{:S(2)}) copy-start(s32[8]{0:T(128)} %param.9) | copy-start | bytes 100
  634.0 24.2 %collective-permute-start = (bf16[3,2,32,2048]{3,2,1,0:T(8,128)(2,1)}, bf16[3,2,32,2048]{3,2,1,0:T(8,128)(2,1)S(1)}, u32[]{:S(2)}, u32[]{:S(2)}) collective-permute-start(bf16[3,2,32,2048]{3,2,1,0:T(8,128)(2,1)} %get-tuple-element.22), channel_id=1, source_target_pairs={{2,0},{3,1},{4,2},{5,3},{6,4},{7,5},{10,8},{11,9},{12,10},{13,11},... | collective-permute-start | bytes 2359304 | tf_op jit(solution)/shard_map/ppermute | solution.py:27
  638.3 41.7 %collective-permute-start.1 = (bf16[3,2,32,2048]{3,2,1,0:T(8,128)(2,1)}, bf16[3,2,32,2048]{3,2,1,0:T(8,128)(2,1)S(1)}, u32[]{:S(2)}, u32[]{:S(2)}) collective-permute-start(bf16[3,2,32,2048]{3,2,1,0:T(8,128)(2,1)} %get-tuple-element.21), channel_id=1, source_target_pairs={{1,0},{2,1},{3,2},{4,3},{5,4},{6,5},{7,6},{9,8},{10,9},{11,10},{12... | collective-permute-start | bytes 2359304 | tf_op jit(solution)/shard_map/ppermute | solution.py:27
  647.0 37.1 %collective-permute-start.2 = (bf16[3,2,32,2048]{3,2,1,0:T(8,128)(2,1)}, bf16[3,2,32,2048]{3,2,1,0:T(8,128)(2,1)S(1)}, u32[]{:S(2)}, u32[]{:S(2)}) collective-permute-start(bf16[3,2,32,2048]{3,2,1,0:T(8,128)(2,1)} %get-tuple-element.20), channel_id=1, source_target_pairs={{0,1},{1,2},{2,3},{3,4},{4,5},{5,6},{6,7},{8,9},{9,10},{10,11},{11... | collective-permute-start | bytes 2359304 | tf_op jit(solution)/shard_map/ppermute | solution.py:27
  648.9 35.1 %collective-permute-start.3 = (bf16[3,2,32,2048]{3,2,1,0:T(8,128)(2,1)}, bf16[3,2,32,2048]{3,2,1,0:T(8,128)(2,1)S(1)}, u32[]{:S(2)}, u32[]{:S(2)}) collective-permute-start(bf16[3,2,32,2048]{3,2,1,0:T(8,128)(2,1)} %get-tuple-element.19), channel_id=1, source_target_pairs={{0,2},{1,3},{2,4},{3,5},{4,6},{5,7},{8,10},{9,11},{10,12},{11,13},... | collective-permute-start | bytes 2359304 | tf_op jit(solution)/shard_map/ppermute | solution.py:27
  658.2 26.4 %copy-start = (bf16[3,2,32,2048]{3,2,1,0:T(8,128)(2,1)}, bf16[3,2,32,2048]{3,2,1,0:T(8,128)(2,1)S(1)}, u32[]{:S(2)}) copy-start(bf16[3,2,32,2048]{3,2,1,0:T(8,128)(2,1)S(1)} %collective-permute-done.refs_0_) | copy-start | bytes 2359300
  680.0 4.6 copy-start.1
  684.0 0.9 copy-start.2
  684.0 1.1 copy-start.3
